TPU v7x, 32 devices: a whole 2x2x4 slice. The times are simulated.
32 devices in a mesh: seq: 8 (over z, x), hx: 4 (over y, core).
Axes of the slice: x: 2, y: 2, z: 4, core: 2. Of those that a mesh axis runs over, the one named last changes fastest.
Arguments:
- query: bfloat16 [8192, 8192], P('seq', 'hx'), may hold values from -6 to 6
- key_in: bfloat16 [8192, 8192], P('seq', 'hx'), may hold values from -6 to 6
- value: bfloat16 [8192, 8192], P('seq', 'hx'), may hold values from -6 to 6
- head_gain: float32 [8192], P('hx'), may hold values from 0.1 to 1.9
- out_weight: bfloat16 [8192, 6144], P('hx', 'seq'), may hold values from -0.0625 to 0.0625
- residual: bfloat16 [8192, 6144], P(('seq', 'hx')), may hold values from -6 to 6
Outputs:
- mixed: bfloat16 [8192, 6144], P(('seq', 'hx'))
All inputs are finite; a program needn't handle non-finite values.
Results may differ from a plain program's by a relative error of at most 0.014.
Values may be sent and summed in bfloat16 or wider, within the bound.
A program may use at most 128 MiB of HBM per device.

v0:
```python
import jax
import jax.numpy as jnp
from jax import lax
from jax.sharding import PartitionSpec as P

DH = 128


def entering(x, axis, combine, identity):
    size, position = (lax.axis_size(axis), lax.axis_index(axis))
    everything = lax.all_gather(x.astype(jnp.bfloat16), axis)
    start = jnp.broadcast_to(jnp.asarray(identity, x.dtype), x.shape)

    def turn(k, before):
        reached = k < position
        new = combine(before, everything[k].astype(x.dtype))
        return jnp.where(reached, new, before)

    return lax.fori_loop(0, size, turn, start)


def activate(array):
    return jax.nn.silu(array.astype(jnp.float32)).astype(jnp.bfloat16)


def per_device(query, key_in, value, head_gain, out_weight, residual):
    highest = lax.Precision.HIGHEST
    tokens_here, width = query.shape
    heads = width // DH
    q_act = activate(query).reshape(tokens_here, heads, DH)
    k_act = activate(key_in).reshape(tokens_here, heads, DH)
    v_heads = value.reshape(tokens_here, heads, DH)
    blocks = min(512, tokens_here)
    count = tokens_here // blocks
    rows = jnp.arange(blocks, dtype=jnp.int32)
    lower = rows[:, None] >= rows[None, :]
    running = jnp.zeros((heads, DH, DH), jnp.float32)
    pieces = []
    for index in range(count):
        q_part = q_act[index * blocks : (index + 1) * blocks]
        k_part = k_act[index * blocks : (index + 1) * blocks]
        v_part = v_heads[index * blocks : (index + 1) * blocks]
        scores = jnp.einsum("thd,shd->hts", q_part, k_part, preferred_element_type=jnp.float32)
        scores = jnp.where(lower[None, :, :], scores, jnp.zeros_like(scores))
        inner = jnp.einsum("hts,she->the", scores, v_part.astype(jnp.float32), precision=highest)
        if index > 0:
            inner = inner + jnp.einsum(
                "thd,hde->the", q_part.astype(jnp.float32), running, precision=highest
            )
        pieces.append(inner)
        running = running + jnp.einsum(
            "thd,the->hde", k_part, v_part, preferred_element_type=jnp.float32
        )
    local_part = jnp.concatenate(pieces, axis=0)
    empty = jnp.zeros((heads, DH, DH), jnp.float32)

    def combine(earlier, later):
        return earlier + later

    prefix = entering(running, "seq", combine, empty)
    attended = local_part + jnp.einsum(
        "thd,hde->the", q_act.astype(jnp.float32), prefix, precision=highest
    )
    meansq = jnp.mean(attended * attended, axis=-1, keepdims=True)
    normed = attended * lax.rsqrt(meansq + 1e-06) * head_gain.reshape(heads, DH)
    normed = normed.astype(jnp.bfloat16).reshape(tokens_here, width)
    full_weight = lax.all_gather(out_weight, "seq", axis=1, tiled=True)
    summed = lax.psum_scatter(
        jnp.dot(normed, full_weight, preferred_element_type=jnp.float32).astype(jnp.bfloat16),
        "hx",
        scatter_dimension=0,
        tiled=True,
    ).astype(jnp.float32)
    return (summed + residual.astype(jnp.float32)).astype(jnp.bfloat16)


def solution(mesh):
    return jax.shard_map(
        per_device,
        mesh=mesh,
        in_specs=(
            P("seq", "hx"),
            P("seq", "hx"),
            P("seq", "hx"),
            P("hx"),
            P("hx", "seq"),
            P(("seq", "hx"), None),
        ),
        out_specs=P(("seq", "hx"), None),
        check_vma=False,
    )
```

profile of v0, /device:TPU:0, one launch (start us, length us, event | category | flops | bytes accessed | tf_op | source)
XLA Modules:
  0.0 733.0 jit_solution(13041921529370957699)
XLA Ops:
  6.5 0.0 all-gather.6.cloned.1.call-start
  6.5 6.4 copy.48
  12.9 4.1 fusion.11
  17.0 0.0 copy-start.8
  17.0 2.4 fusion.24
  19.4 1.3 copy-done.8
  20.7 1.8 fusion.23
  22.5 2.5 copy.81
  25.0 2.9 copy.80
  27.9 0.0 copy-start.2
  27.9 0.0 copy-start.3
  27.9 2.4 fusion.27
  30.4 0.0 copy-start.6
  30.4 1.0 copy-done.6
  31.4 0.0 copy-done.2
  31.4 0.0 copy-done.3
  31.4 1.5 fusion.19
  32.9 0.0 all-gather.6.cloned.1.call-update
  32.9 0.0 all-gather.4.cloned.1.call-start
  33.0 0.7 all-gather.4.cloned.1.call-update
  33.7 0.2 reduce-scatter.2.cloned.1.call-start
  33.9 6.4 copy.47
  40.3 0.1 iota_compare_fusion
  40.4 4.1 fusion.7
  44.4 0.0 copy-start
  44.4 0.0 copy-start.4
  44.5 1.6 fusion.22
  46.1 1.2 copy-done
  47.2 0.0 copy-start.5
  47.2 1.3 copy-done.5
  48.6 0.0 copy-done.4
  48.6 2.4 fusion.26
  50.9 11.2 %fusion = f32[16,512,128]{2,1,0:T(8,128)} fusion(bf16[512,16,128]{0,2,1:T(8,128)(2,1)} %bitcast.44, f32[16,512,512]{2,1,0:T(8,128)S(1)} %fusion.26, pred[512,512]{1,0:T(8,128)(4,1)S(1)} %iota_compare_fusion), kind=kOutput, calls=%fused_computation.1 | convolution fusion | flops 6446645248 | bytes 23330816 | tf_op jit(solution)/shard_map/hts,she->the/dot_general | solution.py:45
  62.1 0.0 copy-start.1
  62.1 0.0 copy-start.7
  62.2 7.3 %bitcast_add_fusion = f32[512,16,128]{2,0,1:T(8,128)} fusion(f32[16,512,128]{2,1,0:T(8,128)} %fusion, f32[16,128,128]{2,1,0:T(8,128)} %copy-done.6, bf16[512,16,128]{0,2,1:T(8,128)(2,1)} %bitcast.49), kind=kOutput, calls=%fused_computation.26 | convolution fusion | flops 1611661312 | bytes 11534336 | tf_op jit(solution)/shard_map/thd,hde->the/dot_general | solution.py:47
  69.5 0.0 copy-done.1
  69.5 0.0 copy-done.7
  69.5 2.4 fusion.25
  71.9 10.0 %fusion.16 = f32[512,16,128]{2,0,1:T(8,128)} fusion(bf16[512,16,128]{0,2,1:T(8,128)(2,1)S(1)} %bitcast.41, f32[16,512,512]{2,1,0:T(8,128)S(1)} %fusion.25, pred[512,512]{1,0:T(8,128)(4,1)S(1)} %iota_compare_fusion), kind=kOutput, calls=%fused_computation.27 | convolution fusion | flops 6446645248 | bytes 23330816 | tf_op jit(solution)/shard_map/hts,she->the/dot_general | solution.py:45
  81.8 26.7 %all-gather.6.cloned.1.call-done = bf16[128,128,128]{2,1,0:T(8,128)(2,1)} async-done(((bf16[16,128,128]{2,1,0:T(8,128)(2,1)}), bf16[128,128,128]{2,1,0:T(8,128)(2,1)}) %all-gather.6.cloned.1.call-update) | async-done | bytes 4194320 | tf_op jit(solution)/shard_map/all_gather | solution.py:11
  108.6 13.2 %while.14 = (s32[]{:T(128)}, f32[16,128,128]{2,1,0:T(8,128)S(1)}, s32[]{:T(128)}, bf16[8,16,128,128]{3,2,1,0:T(8,128)(2,1)}, s32[]{:T(128)}, /*index=5*/s32[]{:T(128)}) while((s32[]{:T(128)}, f32[16,128,128]{2,1,0:T(8,128)S(1)}, s32[]{:T(128)}, bf16[8,16,128,128]{3,2,1,0:T(8,128)(2,1)}, s32[]{:T(128)}, /*index=5*/s32[]{:T(128)}) %tuple.45), condition=%wide.region_1.2_spmd.clone, body=%wide.region_0.1_spmd.clone.sunk | while | flops 1048580 | bytes 2621533 | solution.py:19
  108.6 1.6 add_select_fusion.2
  110.2 1.6 add_select_fusion.2
  111.9 1.6 add_select_fusion.2
  113.5 1.6 add_select_fusion.2
  115.1 1.7 add_select_fusion.2
  116.8 1.7 add_select_fusion.2
  118.5 1.6 add_select_fusion.2
  120.2 1.6 add_select_fusion.2
  121.8 0.0 copy-start.10
  121.8 11.0 %multiply_reduce_fusion = (f32[1024,16]{0,1:T(8,128)S(1)}, f32[1024,16,128]{2,0,1:T(8,128)}) fusion(f32[16,128,128]{2,1,0:T(8,128)S(1)} %get-tuple-element.84, bf16[1024,16,128]{0,2,1:T(8,128)(2,1)} %bitcast.39, f32[512,16,128]{2,0,1:T(8,128)} %bitcast_add_fusion, f32[512,16,128]{2,0,1:T(8,128)} %fusion.16), kind=kOutput, calls=%fused_computation.20 | convolution fusion | flops 3229597696 | bytes 22085632 | tf_op jit(solution)/shard_map/thd,hde->the/dot_general | solution.py:61
  132.8 0.0 copy-done.10
  132.8 6.9 multiply_convert_fusion
  139.7 6.4 copy.65
  146.1 442.9 %all-gather.4.cloned.1.call-done = bf16[2048,6144]{1,0:T(8,128)(2,1)} async-done(((bf16[2048,768]{1,0:T(8,128)(2,1)}), bf16[2048,6144]{1,0:T(8,128)(2,1)}) %all-gather.4.cloned.1.call-update) | async-done | bytes 25165840 | tf_op jit(solution)/shard_map/all_gather | solution.py:67
  589.1 32.9 %convolution_convert_fusion = bf16[1024,6144]{1,0:T(8,128)(2,1)} fusion(bf16[1024,2048]{0,1:T(8,128)(2,1)} %bitcast.51, bf16[2048,6144]{1,0:T(8,128)(2,1)} %all-gather.4.cloned.1.call-done), kind=kOutput, calls=%fused_computation.5 | convolution fusion | flops 25776095232 | bytes 41943040 | tf_op jit(solution)/shard_map/dot_general | solution.py:69
  622.0 0.0 copy-start.9
  622.0 0.0 reduce-scatter.2.cloned.1.call-update
  622.0 99.7 %reduce-scatter.2.cloned.1.call-done = bf16[256,6144]{1,0:T(8,128)(2,1)} async-done(((bf16[1024,6144]{1,0:T(8,128)(2,1)}), bf16[256,6144]{1,0:T(8,128)(2,1)}) %reduce-scatter.2.cloned.1.call-update) | async-done | bytes 3145744 | tf_op jit(solution)/shard_map/reduce_scatter | solution.py:68
  721.7 0.0 copy-done.9
  721.7 4.7 add_convert_fusion
  (2 shorter events, 0.0 us)
Async XLA Ops:
  6.5 102.1 %all-gather.6.cloned.1.call-start = ((), (), s32[]{:S(2)}) async-start(), calls=%async_computation.3 | async-start | bytes 4718592 | tf_op jit(solution)/shard_map/all_gather | solution.py:11
  17.0 3.7 copy-start.8
  27.9 3.5 copy-start.2
  27.9 3.5 copy-start.3
  30.4 1.0 copy-start.6
  32.9 556.1 %all-gather.4.cloned.1.call-start = ((), (), s32[]{:S(2)}) async-start(), calls=%async_computation.1 | async-start | bytes 28311552 | tf_op jit(solution)/shard_map/all_gather | solution.py:67
  33.7 688.1 %reduce-scatter.2.cloned.1.call-start = ((), (), s32[]{:S(2)}) async-start(), calls=%async_computation.2 | async-start | bytes 15728640 | tf_op jit(solution)/shard_map/reduce_scatter | solution.py:68
  44.4 2.8 copy-start
  44.4 4.1 copy-start.4
  47.2 1.3 copy-start.5
  62.1 7.4 %copy-start.1 = (bf16[512,2048]{0,1:T(8,128)(2,1)S(1)}, bf16[512,2048]{0,1:T(8,128)(2,1)}, u32[]{:S(2)}) copy-start(bf16[512,2048]{0,1:T(8,128)(2,1)} %get-tuple-element.112) | copy-start | bytes 6291460
  62.1 7.4 %copy-start.7 = (bf16[512,2048]{0,1:T(8,128)(2,1)S(1)}, bf16[512,2048]{0,1:T(8,128)(2,1)}, u32[]{:S(2)}) copy-start(bf16[512,2048]{0,1:T(8,128)(2,1)} %get-tuple-element.108) | copy-start | bytes 6291460
  121.8 11.0 %copy-start.10 = (f32[2048]{0:T(1024)S(1)}, f32[2048]{0:T(1024)}, u32[]{:S(2)}) copy-start(f32[2048]{0:T(1024)} %param.11) | copy-start | bytes 24580
  622.0 99.8 %copy-start.9 = (bf16[256,6144]{1,0:T(8,128)(2,1)S(1)}, bf16[256,6144]{1,0:T(8,128)(2,1)}, u32[]{:S(2)}) copy-start(bf16[256,6144]{1,0:T(8,128)(2,1)} %param.13) | copy-start | bytes 9437188
Sparse Core Ops, SparseCore 0:
  33.0 75.4 all-gather.5
  110.1 478.8 all-gather.3
  622.1 99.5 reduce-scatter.1
where the time goes:
time: 734 us; the launch traced here: 733 us
  waiting for transfers between devices  570 us (78%)
  matrix products  81.1 us (11%)
  local copies, waits for them, and re-layouts  35.2 us (5%)
  other arithmetic  32.9 us (4%)
  between operations  13.3 us (2%)
    all_gather x1, waiting for transfers between devices, per_device(): full_weight = lax.all_gather(out_weight, 'seq', axis=1, tiled=True)  443 us
    reduce_scatter x1, waiting for transfers between devices, per_device(): lax.psum_scatter(jnp.dot(normed, full_weight, preferred_element_type=jnp....  99.7 us
    dot_general x1, matrix products, per_device(): jnp.dot(normed, full_weight, preferred_element_type=jnp.float32)  32.9 us
    all_gather x1, waiting for transfers between devices, entering(): everything = lax.all_gather(x.astype(jnp.bfloat16), axis)  26.7 us
    unnamed x26, local copies, waits for them, and re-layouts  22.9 us
    dot_general x2, matrix products, per_device(): jnp.einsum('hts,she->the', scores, v_part.astype(jnp.float32), precision=...  21.2 us
  transfers between devices with their start and end apart: 3, of which 3 were waited for; matrix products, arithmetic and copies ran while one was open for 11% of the time, Pallas kernels for 0%

commit v1 on v0

--- a/solution.py
+++ b/solution.py
@@ -4,6 +4,18 @@
 from jax.sharding import PartitionSpec as P
 
 DH = 128
+
+
+def collect(value, axis, dim):
+    ways, here = (lax.axis_size(axis), lax.axis_index(axis))
+    grown, reach = (value, 1)
+    while reach < ways:
+        theirs = lax.ppermute(grown, axis, [(d, d ^ reach) for d in range(ways)])
+        mine_first = jnp.concatenate([grown, theirs], axis=dim)
+        theirs_first = jnp.concatenate([theirs, grown], axis=dim)
+        grown = jnp.where(here & reach == 0, mine_first, theirs_first)
+        reach = 2 * reach
+    return grown
 
 
 def entering(x, axis, combine, identity):
@@ -64,7 +76,7 @@
     meansq = jnp.mean(attended * attended, axis=-1, keepdims=True)
     normed = attended * lax.rsqrt(meansq + 1e-06) * head_gain.reshape(heads, DH)
     normed = normed.astype(jnp.bfloat16).reshape(tokens_here, width)
-    full_weight = lax.all_gather(out_weight, "seq", axis=1, tiled=True)
+    full_weight = collect(out_weight, "seq", 1)
     summed = lax.psum_scatter(
         jnp.dot(normed, full_weight, preferred_element_type=jnp.float32).astype(jnp.bfloat16),
         "hx",

time: 734 us -> 984 us (1.34)
  waiting for transfers between devices: 570 us -> 783 us
  other arithmetic: 32.9 us -> 57.4 us
    all_gather x1 -> x0, waiting for transfers between devices: 443 us -> none  [per_device(): full_weight = lax.all_gather(out_weight, 'seq', axis=1, tiled=True)]
    ppermute x0 -> x3, waiting for transfers between devices: none -> 389 us  [collect(): theirs = lax.ppermute(grown, axis, [(d, d ^ reach) for d in range(ways)])]
    all_gather x1, waiting for transfers between devices: 26.7 us -> 293 us  [entering(): everything = lax.all_gather(x.astype(jnp.bfloat16), axis)]
    select_n x0 -> x2, other arithmetic: none -> 23.2 us  [collect(): grown = jnp.where(here & reach == 0, mine_first, theirs_first)]
    unnamed x26 -> x28, local copies, waits for them, and re-layouts: 22.9 us -> 22.2 us
  transfers between devices with their start and end apart: 3 -> 5, of which waited for: 3 -> 5; matrix products, arithmetic and copies ran while one was open for 11% -> 11% of each run, Pallas kernels for 0% -> 0%
where the time goes in v1:
time: 984 us; the launch traced here: 983 us
  waiting for transfers between devices  783 us (80%)
  matrix products  86.9 us (9%)
  other arithmetic  57.4 us (6%)
  local copies, waits for them, and re-layouts  34.7 us (4%)
  between operations  13.5 us (1%)
    ppermute x3, waiting for transfers between devices, collect(): theirs = lax.ppermute(grown, axis, [(d, d ^ reach) for d in range(ways)])  389 us
    all_gather x1, waiting for transfers between devices, entering(): everything = lax.all_gather(x.astype(jnp.bfloat16), axis)  293 us
    reduce_scatter x1, waiting for transfers between devices, per_device(): lax.psum_scatter(jnp.dot(normed, full_weight, preferred_element_type=jnp....  101 us
    dot_general x1, matrix products, per_device(): jnp.dot(normed, full_weight, preferred_element_type=jnp.float32)  40.4 us
    select_n x2, other arithmetic, collect(): grown = jnp.where(here & reach == 0, mine_first, theirs_first)  23.2 us
    unnamed x28, local copies, waits for them, and re-layouts  22.2 us
    dot_general x2, matrix products, per_device(): jnp.einsum('hts,she->the', scores, v_part.astype(jnp.float32), precision=...  21.2 us
  transfers between devices with their start and end apart: 5, of which 5 were waited for; matrix products, arithmetic and copies ran while one was open for 11% of the time, Pallas kernels for 0%

profile of v1, /device:TPU:0, one launch (start us, length us, event | category | flops | bytes accessed | tf_op | source)
XLA Modules:
  0.0 982.9 jit_solution(1297650419907339148)
XLA Ops:
  6.5 0.0 all-gather.3.cloned.1.call-start
  6.5 3.0 collective-permute-start
  9.5 68.3 %collective-permute-done = bf16[2048,768]{1,0:T(8,128)(2,1)S(1)} collective-permute-done((bf16[2048,768]{1,0:T(8,128)(2,1)}, bf16[2048,768]{1,0:T(8,128)(2,1)S(1)}, u32[]{:S(2)}, u32[]{:S(2)}) %collective-permute-start) | collective-permute-done | bytes 3145760 | tf_op jit(solution)/shard_map/ppermute | solution.py:13
  77.8 7.6 maximum_select_fusion.5
  85.4 1.8 collective-permute-start.1
  87.3 6.3 copy.48
  93.6 5.4 fusion.19
  99.0 123.4 %collective-permute-done.1 = bf16[2048,1536]{1,0:T(8,128)(2,1)} collective-permute-done((bf16[2048,1536]{1,0:T(8,128)(2,1)}, bf16[2048,1536]{1,0:T(8,128)(2,1)}, u32[]{:S(2)}, u32[]{:S(2)}) %collective-permute-start.1) | collective-permute-done | bytes 6291488 | tf_op jit(solution)/shard_map/ppermute | solution.py:13
  222.4 15.6 %maximum_select_fusion.2 = bf16[2048,3072]{1,0:T(8,128)(2,1)} fusion(bf16[2048,1536]{1,0:T(8,128)(2,1)} %collective-permute-done.1, bf16[2048,1536]{1,0:T(8,128)(2,1)} %maximum_select_fusion.5, pred[]{:T(512)S(6)} %eq.10), kind=kLoop, calls=%fused_computation.13 | loop fusion | flops 56623104 | bytes 25165824 | tf_op jit(solution)/shard_map/jit(_where)/select_n | solution.py:16
  238.0 2.6 collective-permute-start.2
  240.6 0.0 copy-done.9
  240.6 1.7 fusion.32
  242.3 2.5 copy.81
  244.9 2.9 copy.80
  247.7 0.0 copy-start.3
  247.7 2.6 fusion.33
  250.4 0.0 copy-start.1
  250.4 0.0 copy-start.4
  250.4 1.3 copy-done.1
  251.7 0.7 fusion.36
  252.4 0.0 copy-start.7
  252.4 0.0 copy-done.4
  252.5 1.0 copy-done.7
  253.4 0.0 copy-done.3
  253.4 1.5 fusion.27
  254.9 0.0 all-gather.3.cloned.1.call-update
  255.0 0.2 reduce-scatter.2.cloned.1.call-start
  255.2 6.4 copy.47
  261.6 0.1 iota_compare_fusion
  261.7 4.2 fusion.15
  265.9 0.0 copy-start
  265.9 0.0 copy-start.5
  265.9 1.6 fusion.31
  267.5 1.2 copy-done
  268.7 0.6 copy-done.6
  269.3 0.0 copy-done.5
  269.3 2.4 fusion.35
  271.7 11.2 %fusion.7 = f32[16,512,128]{2,1,0:T(8,128)} fusion(bf16[512,16,128]{0,2,1:T(8,128)(2,1)} %bitcast.44, f32[16,512,512]{2,1,0:T(8,128)S(1)} %fusion.35, pred[512,512]{1,0:T(8,128)(4,1)S(1)} %iota_compare_fusion), kind=kOutput, calls=%fused_computation.9 | convolution fusion | flops 6446645248 | bytes 23330816 | tf_op jit(solution)/shard_map/hts,she->the/dot_general | solution.py:57
  282.9 7.3 bitcast_add_fusion
  290.3 0.0 copy-done.2
  290.3 0.0 copy-done.8
  290.3 2.4 fusion.34
  292.6 10.0 %fusion.24 = f32[512,16,128]{2,0,1:T(8,128)} fusion(bf16[512,16,128]{0,2,1:T(8,128)(2,1)S(1)} %bitcast.41, f32[16,512,512]{2,1,0:T(8,128)S(1)} %fusion.34, pred[512,512]{1,0:T(8,128)(4,1)S(1)} %iota_compare_fusion), kind=kOutput, calls=%fused_computation.37 | convolution fusion | flops 6446645248 | bytes 23330816 | tf_op jit(solution)/shard_map/hts,she->the/dot_general | solution.py:57
  302.6 293.4 %all-gather.3.cloned.1.call-done = bf16[128,128,128]{2,1,0:T(8,128)(2,1)} async-done(((bf16[16,128,128]{2,1,0:T(8,128)(2,1)}), bf16[128,128,128]{2,1,0:T(8,128)(2,1)}) %all-gather.3.cloned.1.call-update) | async-done | bytes 4194320 | tf_op jit(solution)/shard_map/all_gather | solution.py:23
  596.0 13.1 %while.14 = (s32[]{:T(128)}, f32[16,128,128]{2,1,0:T(8,128)S(1)}, s32[]{:T(128)}, bf16[8,16,128,128]{3,2,1,0:T(8,128)(2,1)}, s32[]{:T(128)}, /*index=5*/s32[]{:T(128)}) while((s32[]{:T(128)}, f32[16,128,128]{2,1,0:T(8,128)S(1)}, s32[]{:T(128)}, bf16[8,16,128,128]{3,2,1,0:T(8,128)(2,1)}, s32[]{:T(128)}, /*index=5*/s32[]{:T(128)}) %tuple.43), condition=%wide.region_1.2_spmd.clone, body=%wide.region_0.1_spmd.clone.sunk | while | flops 1048580 | bytes 2621533 | solution.py:31
  596.0 1.6 add_select_fusion.2
  597.7 1.6 add_select_fusion.2
  599.3 1.6 add_select_fusion.2
  600.9 1.6 add_select_fusion.2
  602.6 1.6 add_select_fusion.2
  604.2 1.6 add_select_fusion.2
  605.9 1.6 add_select_fusion.2
  607.5 1.6 add_select_fusion.2
  609.1 0.0 copy-start.11
  609.1 11.0 %multiply_reduce_fusion = (f32[1024,16]{0,1:T(8,128)S(1)}, f32[1024,16,128]{2,0,1:T(8,128)}) fusion(f32[16,128,128]{2,1,0:T(8,128)S(1)} %get-tuple-element.84, bf16[1024,16,128]{0,2,1:T(8,128)(2,1)} %bitcast.39, f32[512,16,128]{2,0,1:T(8,128)} %bitcast_add_fusion, f32[512,16,128]{2,0,1:T(8,128)} %fusion.24), kind=kOutput, calls=%fused_computation.29 | convolution fusion | flops 3229597696 | bytes 22085632 | tf_op jit(solution)/shard_map/thd,hde->the/dot_general | solution.py:73
  620.1 0.0 copy-done.11
  620.1 6.9 multiply_convert_fusion
  627.0 6.4 copy.65
  633.5 196.8 %collective-permute-done.2 = bf16[2048,3072]{1,0:T(8,128)(2,1)} collective-permute-done((bf16[2048,3072]{1,0:T(8,128)(2,1)}, bf16[2048,3072]{1,0:T(8,128)(2,1)}, u32[]{:S(2)}, u32[]{:S(2)}) %collective-permute-start.2) | collective-permute-done | bytes 12582944 | tf_op jit(solution)/shard_map/ppermute | solution.py:13
  830.3 40.4 %fusion.11 = bf16[1024,6144]{1,0:T(8,128)(2,1)} fusion(bf16[1024,2048]{0,1:T(8,128)(2,1)} %bitcast.51, bf16[2048,3072]{1,0:T(8,128)(2,1)} %collective-permute-done.2, bf16[2048,3072]{1,0:T(8,128)(2,1)} %maximum_select_fusion.2, pred[]{:T(512)S(6)} %eq.9), kind=kOutput, calls=%fused_computation.14 | convolution fusion | flops 25889341440 | bytes 41943040 | tf_op jit(solution)/shard_map/dot_general | solution.py:81
  870.7 0.0 reduce-scatter.2.cloned.1.call-update
  870.7 100.6 %reduce-scatter.2.cloned.1.call-done = bf16[256,6144]{1,0:T(8,128)(2,1)} async-done(((bf16[1024,6144]{1,0:T(8,128)(2,1)}), bf16[256,6144]{1,0:T(8,128)(2,1)}) %reduce-scatter.2.cloned.1.call-update) | async-done | bytes 3145744 | tf_op jit(solution)/shard_map/reduce_scatter | solution.py:80
  971.3 0.0 copy-done.10
  971.3 4.7 add_convert_fusion
  (7 shorter events, 0.0 us)
Async XLA Ops:
  6.5 589.5 %all-gather.3.cloned.1.call-start = ((), (), s32[]{:S(2)}) async-start(), calls=%async_computation.2 | async-start | bytes 4718592 | tf_op jit(solution)/shard_map/all_gather | solution.py:23
  6.5 71.3 %collective-permute-start = (bf16[2048,768]{1,0:T(8,128)(2,1)}, bf16[2048,768]{1,0:T(8,128)(2,1)S(1)}, u32[]{:S(2)}, u32[]{:S(2)}) collective-permute-start(bf16[2048,768]{1,0:T(8,128)(2,1)} %param.12), channel_id=1, source_target_pairs={{0,4},{4,0},{8,12},{12,8},{16,20},{20,16},{24,28},{28,24},{1,5},{5... | collective-permute-start | bytes 9437192 | tf_op jit(solution)/shard_map/ppermute | solution.py:13
  85.4 137.0 %collective-permute-start.1 = (bf16[2048,1536]{1,0:T(8,128)(2,1)}, bf16[2048,1536]{1,0:T(8,128)(2,1)}, u32[]{:S(2)}, u32[]{:S(2)}) collective-permute-start(bf16[2048,1536]{1,0:T(8,128)(2,1)} %maximum_select_fusion.5), channel_id=1, source_target_pairs={{0,8},{4,12},{8,0},{12,4},{16,24},{20,28},{24,16},{28,20},{1,9},{5... | collective-permute-start | bytes 18874376 | tf_op jit(solution)/shard_map/ppermute | solution.py:13
  99.0 141.6 %copy-start.9 = (bf16[1024,2048]{1,0:T(8,128)(2,1)S(1)}, bf16[1024,2048]{1,0:T(8,128)(2,1)}, u32[]{:S(2)}) copy-start(bf16[1024,2048]{1,0:T(8,128)(2,1)} %param.10) | copy-start | bytes 12582916
  238.0 592.3 %collective-permute-start.2 = (bf16[2048,3072]{1,0:T(8,128)(2,1)}, bf16[2048,3072]{1,0:T(8,128)(2,1)}, u32[]{:S(2)}, u32[]{:S(2)}) collective-permute-start(bf16[2048,3072]{1,0:T(8,128)(2,1)} %maximum_select_fusion.2), channel_id=1, source_target_pairs={{0,16},{4,20},{8,24},{12,28},{16,0},{20,4},{24,8},{28,12},{1,17},{... | collective-permute-start | bytes 37748744 | tf_op jit(solution)/shard_map/ppermute | solution.py:13
  247.7 5.7 copy-start.3
  250.4 1.3 copy-start.1
  250.4 2.1 copy-start.4
  252.4 1.0 copy-start.7
  255.0 716.3 %reduce-scatter.2.cloned.1.call-start = ((), (), s32[]{:S(2)}) async-start(), calls=%async_computation.1 | async-start | bytes 15728640 | tf_op jit(solution)/shard_map/reduce_scatter | solution.py:80
  265.9 2.8 copy-start
  265.9 3.4 copy-start.5
  267.5 1.8 copy-start.6
  282.9 7.3 copy-start.2
  282.9 7.4 copy-start.8
  609.1 11.0 %copy-start.11 = (f32[2048]{0:T(1024)S(1)}, f32[2048]{0:T(1024)}, u32[]{:S(2)}) copy-start(f32[2048]{0:T(1024)} %param.11) | copy-start | bytes 24580
  870.7 100.6 %copy-start.10 = (bf16[256,6144]{1,0:T(8,128)(2,1)S(1)}, bf16[256,6144]{1,0:T(8,128)(2,1)}, u32[]{:S(2)}) copy-start(bf16[256,6144]{1,0:T(8,128)(2,1)} %param.13) | copy-start | bytes 9437188
Sparse Core Ops, SparseCore 0:
  255.1 340.8 all-gather.2
  870.9 100.3 reduce-scatter.1
